TPU v7x, 32 devices: a whole 2x2x4 slice. The times are simulated.
32 devices in a mesh: scen: 2 (over y), dw: 4 (over x, core), reg: 4 (over z).
Axes of the slice: x: 2, y: 2, z: 4, core: 2. Of those that a mesh axis runs over, the one named last changes fastest.
Arguments:
- load_base: float32 [96, 65536], P(None, ('scen', 'dw', 'reg')), parts along dimension 1, may hold values from -24 to 24
- kkt_inverse: float32 [64, 96, 96], replicated, may hold values from -1 to 2
- archetype: int32 [65536], P(('scen', 'dw', 'reg')), parts along dimension 0, may hold values from 0 to 63
- feeder: int32 [65536], P(('scen', 'dw', 'reg')), parts along dimension 0, may hold values from 0 to 255, as said below
- live_counts: int32 [32, 4], P(('scen', 'dw', 'reg')), parts along dimension 0, may hold values from 1 to 512, as said below
- feeder_cap: int32 [512], P(('scen', 'dw', 'reg')), parts along dimension 0, may hold values from 1000 to 11999
- dual_start: float32 [512, 96], P(('scen', 'dw', 'reg')), parts along dimension 0, may hold values from 0 to 1
- balance_target: float32 [192], P('scen'), parts along dimension 0, may hold values from -6 to 6
Outputs:
- roster: float32 [96, 65536], P(None, ('scen', 'dw', 'reg')), parts along dimension 1
- feeder_duals: float32 [512, 96], P(('scen', 'dw', 'reg')), parts along dimension 0
- balance_dual: float32 [192], P('scen'), parts along dimension 0
There are 2 independent parts, one for each index of `scen`. A program takes and returns all parts, laid end to end along the dimension named above; an argument that names none is the same for every part. Nothing has to cross between parts.
Inputs may be any that keep to these rules, and one draw needn't show every extreme that they name: The feeder of the dwelling in slot s of the device at index j along dw and r along reg lies in block k * 4 + r of 16 feeders, where k = s // 512. `live_counts`: row d (devices in the order dw+reg) gives for each block k the number of leading slots of that block that hold a dwelling; the other slots are empty. Every row has a block of 512.
All inputs are finite; a program needn't handle non-finite values.
Results may differ from a plain program's by a relative error of at most 0.0003.
Values sent between devices are 32-bit elements; how exact they have to be, the bound alone decides.
No kernel may reach another device: no remote copies, remote signals or barrier semaphores. Data moves between devices by JAX's collectives and lax.ppermute only.
A program may use at most 64 MiB of HBM per device.

v0:
```python
import math
import jax
import jax.numpy as jnp
from jax import lax
from jax.sharding import PartitionSpec as P

ITERS = 2
rho_weight = 0.5
dual_rate = 0.1
balance_rate = 1.0


def apply_inverse(kkt_inverse, archetype, rhs_field, block_width):
    steps_count, rows_count = rhs_field.shape
    block_count = rows_count // block_width
    blocks_in = rhs_field.reshape(steps_count, block_count, block_width).transpose(1, 0, 2)
    labels_in = archetype.reshape(block_count, block_width)

    def one_block(operand):
        labels, columns_in = operand
        picked = jnp.take(kkt_inverse, labels, axis=0)
        return jnp.einsum("bts,sb->tb", picked, columns_in, precision=lax.Precision.HIGHEST)

    out_blocks = lax.map(one_block, (labels_in, blocks_in))
    return out_blocks.transpose(1, 0, 2).reshape(steps_count, rows_count)


def on_device(
    load_base, kkt_inverse, archetype, feeder, live_counts, feeder_cap, dual_start, balance_target
):
    steps_count, rows_count = load_base.shape
    block_total = lax.axis_size("dw")
    slot_width = rows_count // block_total
    owned_count = dual_start.shape[0]
    slot_index = jnp.arange(slot_width, dtype=jnp.int32)
    live_mask = (
        (live_counts.reshape(block_total, 1) > slot_index[None, :])
        .reshape(rows_count)
        .astype(jnp.float32)
    )
    all_rows = rows_count * block_total * lax.axis_size("reg")
    inv_root = 1.0 / math.sqrt(all_rows)
    block_width = math.gcd(rows_count, 256)
    local_label = feeder % owned_count
    cap_value = feeder_cap.astype(jnp.float32) * 0.001
    feeder_duals = dual_start
    balance_dual = jnp.zeros((steps_count,), jnp.float32)
    roster = jnp.zeros_like(load_base)
    contract_rows = (((0,), (1,)), ((), ()))
    arrived_labels = lax.all_to_all(local_label, "dw", split_axis=0, concat_axis=0, tiled=True)
    owner_table = (
        arrived_labels[:, None] == jnp.arange(owned_count, dtype=jnp.int32)[None, :]
    ).astype(jnp.float32)
    for sweep_index in range(ITERS):
        owner_rows = lax.dot_general(
            feeder_duals, owner_table, contract_rows, precision=lax.Precision.HIGHEST
        )
        dwelling_duals = lax.all_to_all(owner_rows, "dw", split_axis=1, concat_axis=1, tiled=True)
        rhs_field = load_base - dwelling_duals - balance_dual[:, None] + rho_weight * roster
        roster = apply_inverse(kkt_inverse, archetype, rhs_field, block_width) * live_mask[None, :]
        arrived_loads = lax.all_to_all(roster, "dw", split_axis=1, concat_axis=1, tiled=True)
        feeder_loads = lax.dot_general(
            owner_table, arrived_loads, contract_rows, precision=lax.Precision.HIGHEST
        )
        system_load = lax.psum(jnp.sum(feeder_loads, axis=0), ("dw", "reg"))
        feeder_duals = jnp.maximum(
            feeder_duals + dual_rate * (feeder_loads - cap_value[:, None]), 0.0
        )
        balance_dual = balance_dual + balance_rate * (system_load * inv_root - balance_target)
    return (roster, feeder_duals, balance_dual)


def solution(mesh):
    in_specs = (
        P(None, ("scen", "dw", "reg")),
        P(),
        P(("scen", "dw", "reg")),
        P(("scen", "dw", "reg")),
        P(("scen", "dw", "reg"), None),
        P(("scen", "dw", "reg")),
        P(("scen", "dw", "reg"), None),
        P("scen"),
    )
    out_specs = (P(None, ("scen", "dw", "reg")), P(("scen", "dw", "reg"), None), P("scen"))
    return jax.shard_map(
        on_device, mesh=mesh, in_specs=in_specs, out_specs=out_specs, check_vma=False
    )
```

profile of v0, /device:TPU:0, one launch (start us, length us, event | category | flops | bytes accessed | tf_op | source)
XLA Modules:
  0.0 417.4 jit_solution(971037340868108701)
XLA Ops:
  1.3 7.8 %all_to_all.51 = s32[4,512,1]{1,2,0:T(1,128)S(1)} all-to-all(s32[4,512,1]{1,2,0:T(1,128)S(1)} %bitcast.121), channel_id=1, replica_groups=mesh['scen'=2,'dw'=4,'reg'=4] {'dw'}, dimensions={0} | all-to-all | bytes 16384 | tf_op jit(solution)/shard_map/all_to_all | solution.py:50
  16.9 10.2 %all-to-all-done.1 = f32[96,4,512]{2,0,1:T(8,128)S(1)} async-done(((f32[96,4,512]{2,0,1:T(8,128)}), f32[96,4,512]{2,0,1:T(8,128)S(1)}, u32[]{:S(2)}, u32[]{:S(2)}) %all-to-all-start.1) | async-done | bytes 786464 | tf_op jit(solution)/shard_map/all_to_all | solution.py:58
  29.6 136.5 %while.20 = (s32[]{:T(128)}, f32[8,96,256]{2,1,0:T(8,128)}, f32[8,96,256]{2,0,1:T(8,128)S(1)}, s32[8,256]{1,0:T(8,128)S(1)}, f32[64,96,96]{2,1,0:T(8,128)}, /*index=5*/s32[]{:T(128)}) while((s32[]{:T(128)}, f32[8,96,256]{2,1,0:T(8,128)}, f32[8,96,256]{2,0,1:T(8,128)S(1)}, s32[8,256]{1,0:T(8,128)S(1)}, f32[64,96,96]{2,1,0:T(8,128)}, ...), condition=%wide.region_1.3_spmd, body=%wide.region_0.2_spmd.sunk | while | flops 7056642 | bytes 29306956 | solution.py:24
  29.6 7.8 %gather_fusion = f32[256,96,96]{2,1,0:T(8,128)} fusion(f32[64,96,96]{2,1,0:T(8,128)} %get-tuple-element.179, s32[1024]{0:T(1024)S(1)} %pad_clamp_fusion.4), kind=kCustom, calls=%fused_computation.clone.clone.1 | custom fusion | bytes 18875392 | tf_op jit(solution)/shard_map/while/body/eval_jaxpr/jit(_take)/gather | solution.py:21
  37.6 8.3 %multiply_reduce_fusion.4 = f32[256,96]{1,0:T(8,128)S(1)} fusion(f32[256,96,96]{2,1,0:T(8,128)} %gather_fusion, f32[256,96]{1,0:T(8,128)S(1)} %bitcast.87, pred[256]{0:T(512)(128)(4,1)S(1)} %compare_and_fusion.4), kind=kLoop, calls=%fused_computation.2.clone.1 | loop fusion | flops 7053312 | bytes 9634048 | tf_op jit(solution)/shard_map/while
  46.7 7.8 %gather_fusion = f32[256,96,96]{2,1,0:T(8,128)} fusion(f32[64,96,96]{2,1,0:T(8,128)} %get-tuple-element.179, s32[1024]{0:T(1024)S(1)} %pad_clamp_fusion.4), kind=kCustom, calls=%fused_computation.clone.clone.1 | custom fusion | bytes 18875392 | tf_op jit(solution)/shard_map/while/body/eval_jaxpr/jit(_take)/gather | solution.py:21
  54.7 8.3 %multiply_reduce_fusion.4 = f32[256,96]{1,0:T(8,128)S(1)} fusion(f32[256,96,96]{2,1,0:T(8,128)} %gather_fusion, f32[256,96]{1,0:T(8,128)S(1)} %bitcast.87, pred[256]{0:T(512)(128)(4,1)S(1)} %compare_and_fusion.4), kind=kLoop, calls=%fused_computation.2.clone.1 | loop fusion | flops 7053312 | bytes 9634048 | tf_op jit(solution)/shard_map/while
  63.7 7.8 %gather_fusion = f32[256,96,96]{2,1,0:T(8,128)} fusion(f32[64,96,96]{2,1,0:T(8,128)} %get-tuple-element.179, s32[1024]{0:T(1024)S(1)} %pad_clamp_fusion.4), kind=kCustom, calls=%fused_computation.clone.clone.1 | custom fusion | bytes 18875392 | tf_op jit(solution)/shard_map/while/body/eval_jaxpr/jit(_take)/gather | solution.py:21
  71.7 8.3 %multiply_reduce_fusion.4 = f32[256,96]{1,0:T(8,128)S(1)} fusion(f32[256,96,96]{2,1,0:T(8,128)} %gather_fusion, f32[256,96]{1,0:T(8,128)S(1)} %bitcast.87, pred[256]{0:T(512)(128)(4,1)S(1)} %compare_and_fusion.4), kind=kLoop, calls=%fused_computation.2.clone.1 | loop fusion | flops 7053312 | bytes 9634048 | tf_op jit(solution)/shard_map/while
  80.8 7.8 %gather_fusion = f32[256,96,96]{2,1,0:T(8,128)} fusion(f32[64,96,96]{2,1,0:T(8,128)} %get-tuple-element.179, s32[1024]{0:T(1024)S(1)} %pad_clamp_fusion.4), kind=kCustom, calls=%fused_computation.clone.clone.1 | custom fusion | bytes 18875392 | tf_op jit(solution)/shard_map/while/body/eval_jaxpr/jit(_take)/gather | solution.py:21
  88.8 8.3 %multiply_reduce_fusion.4 = f32[256,96]{1,0:T(8,128)S(1)} fusion(f32[256,96,96]{2,1,0:T(8,128)} %gather_fusion, f32[256,96]{1,0:T(8,128)S(1)} %bitcast.87, pred[256]{0:T(512)(128)(4,1)S(1)} %compare_and_fusion.4), kind=kLoop, calls=%fused_computation.2.clone.1 | loop fusion | flops 7053312 | bytes 9634048 | tf_op jit(solution)/shard_map/while
  97.8 7.8 %gather_fusion = f32[256,96,96]{2,1,0:T(8,128)} fusion(f32[64,96,96]{2,1,0:T(8,128)} %get-tuple-element.179, s32[1024]{0:T(1024)S(1)} %pad_clamp_fusion.4), kind=kCustom, calls=%fused_computation.clone.clone.1 | custom fusion | bytes 18875392 | tf_op jit(solution)/shard_map/while/body/eval_jaxpr/jit(_take)/gather | solution.py:21
  105.8 8.3 %multiply_reduce_fusion.4 = f32[256,96]{1,0:T(8,128)S(1)} fusion(f32[256,96,96]{2,1,0:T(8,128)} %gather_fusion, f32[256,96]{1,0:T(8,128)S(1)} %bitcast.87, pred[256]{0:T(512)(128)(4,1)S(1)} %compare_and_fusion.4), kind=kLoop, calls=%fused_computation.2.clone.1 | loop fusion | flops 7053312 | bytes 9634048 | tf_op jit(solution)/shard_map/while
  114.9 7.8 %gather_fusion = f32[256,96,96]{2,1,0:T(8,128)} fusion(f32[64,96,96]{2,1,0:T(8,128)} %get-tuple-element.179, s32[1024]{0:T(1024)S(1)} %pad_clamp_fusion.4), kind=kCustom, calls=%fused_computation.clone.clone.1 | custom fusion | bytes 18875392 | tf_op jit(solution)/shard_map/while/body/eval_jaxpr/jit(_take)/gather | solution.py:21
  122.9 8.3 %multiply_reduce_fusion.4 = f32[256,96]{1,0:T(8,128)S(1)} fusion(f32[256,96,96]{2,1,0:T(8,128)} %gather_fusion, f32[256,96]{1,0:T(8,128)S(1)} %bitcast.87, pred[256]{0:T(512)(128)(4,1)S(1)} %compare_and_fusion.4), kind=kLoop, calls=%fused_computation.2.clone.1 | loop fusion | flops 7053312 | bytes 9634048 | tf_op jit(solution)/shard_map/while
  131.9 7.8 %gather_fusion = f32[256,96,96]{2,1,0:T(8,128)} fusion(f32[64,96,96]{2,1,0:T(8,128)} %get-tuple-element.179, s32[1024]{0:T(1024)S(1)} %pad_clamp_fusion.4), kind=kCustom, calls=%fused_computation.clone.clone.1 | custom fusion | bytes 18875392 | tf_op jit(solution)/shard_map/while/body/eval_jaxpr/jit(_take)/gather | solution.py:21
  140.0 8.3 %multiply_reduce_fusion.4 = f32[256,96]{1,0:T(8,128)S(1)} fusion(f32[256,96,96]{2,1,0:T(8,128)} %gather_fusion, f32[256,96]{1,0:T(8,128)S(1)} %bitcast.87, pred[256]{0:T(512)(128)(4,1)S(1)} %compare_and_fusion.4), kind=kLoop, calls=%fused_computation.2.clone.1 | loop fusion | flops 7053312 | bytes 9634048 | tf_op jit(solution)/shard_map/while
  149.0 7.8 %gather_fusion = f32[256,96,96]{2,1,0:T(8,128)} fusion(f32[64,96,96]{2,1,0:T(8,128)} %get-tuple-element.179, s32[1024]{0:T(1024)S(1)} %pad_clamp_fusion.4), kind=kCustom, calls=%fused_computation.clone.clone.1 | custom fusion | bytes 18875392 | tf_op jit(solution)/shard_map/while/body/eval_jaxpr/jit(_take)/gather | solution.py:21
  157.0 8.3 %multiply_reduce_fusion.4 = f32[256,96]{1,0:T(8,128)S(1)} fusion(f32[256,96,96]{2,1,0:T(8,128)} %gather_fusion, f32[256,96]{1,0:T(8,128)S(1)} %bitcast.87, pred[256]{0:T(512)(128)(4,1)S(1)} %compare_and_fusion.4), kind=kLoop, calls=%fused_computation.2.clone.1 | loop fusion | flops 7053312 | bytes 9634048 | tf_op jit(solution)/shard_map/while
  177.6 11.7 %all-to-all-done.2 = f32[96,4,512]{2,0,1:T(8,128)} async-done(((f32[96,4,512]{2,0,1:T(8,128)}), f32[96,4,512]{2,0,1:T(8,128)}, u32[]{:S(2)}, u32[]{:S(2)}) %all-to-all-start.2) | async-done | bytes 786464 | tf_op jit(solution)/shard_map/all_to_all | solution.py:61
  199.9 34.7 %psum.14 = f32[96]{0:T(128)S(1)} all-reduce(f32[96]{0:T(128)S(1)} %get-tuple-element.99), channel_id=1, replica_groups=mesh['scen'=2,'dw'=4,'reg'=4] {'dw','reg'}, use_global_device_ids=true, to_apply=%region_3.5 | all-reduce | flops 96 | bytes 768 | tf_op jit(solution)/shard_map/psum | solution.py:65
  239.3 127.9 %while.21 = (s32[]{:T(128)}, f32[8,96,256]{2,1,0:T(8,128)}, f32[8,96,256]{2,1,0:T(8,128)}, s32[8,256]{1,0:T(8,128)S(1)}, f32[64,96,96]{2,1,0:T(8,128)S(1)}, /*index=5*/s32[]{:T(128)}) while((s32[]{:T(128)}, f32[8,96,256]{2,1,0:T(8,128)}, f32[8,96,256]{2,1,0:T(8,128)}, s32[8,256]{1,0:T(8,128)S(1)}, f32[64,96,96]{2,1,0:T(8,128)S(1)}, ...), condition=%wide.region_5.7_spmd, body=%wide.region_4.6_spmd.sunk | while | flops 7056642 | bytes 29306956 | solution.py:24
  246.3 8.3 %multiply_reduce_fusion.5 = f32[256,96]{1,0:T(8,128)S(1)} fusion(f32[256,96,96]{2,1,0:T(8,128)} %gather_fusion.1, f32[256,96]{1,0:T(8,128)S(1)} %copy.85, pred[256]{0:T(512)(128)(4,1)S(1)} %compare_and_fusion.5), kind=kLoop, calls=%fused_computation.9.clone.1 | loop fusion | flops 7053312 | bytes 9634048 | tf_op jit(solution)/shard_map/while
  262.3 8.3 %multiply_reduce_fusion.5 = f32[256,96]{1,0:T(8,128)S(1)} fusion(f32[256,96,96]{2,1,0:T(8,128)} %gather_fusion.1, f32[256,96]{1,0:T(8,128)S(1)} %copy.85, pred[256]{0:T(512)(128)(4,1)S(1)} %compare_and_fusion.5), kind=kLoop, calls=%fused_computation.9.clone.1 | loop fusion | flops 7053312 | bytes 9634048 | tf_op jit(solution)/shard_map/while
  278.3 8.3 %multiply_reduce_fusion.5 = f32[256,96]{1,0:T(8,128)S(1)} fusion(f32[256,96,96]{2,1,0:T(8,128)} %gather_fusion.1, f32[256,96]{1,0:T(8,128)S(1)} %copy.85, pred[256]{0:T(512)(128)(4,1)S(1)} %compare_and_fusion.5), kind=kLoop, calls=%fused_computation.9.clone.1 | loop fusion | flops 7053312 | bytes 9634048 | tf_op jit(solution)/shard_map/while
  294.2 8.3 %multiply_reduce_fusion.5 = f32[256,96]{1,0:T(8,128)S(1)} fusion(f32[256,96,96]{2,1,0:T(8,128)} %gather_fusion.1, f32[256,96]{1,0:T(8,128)S(1)} %copy.85, pred[256]{0:T(512)(128)(4,1)S(1)} %compare_and_fusion.5), kind=kLoop, calls=%fused_computation.9.clone.1 | loop fusion | flops 7053312 | bytes 9634048 | tf_op jit(solution)/shard_map/while
  310.2 8.3 %multiply_reduce_fusion.5 = f32[256,96]{1,0:T(8,128)S(1)} fusion(f32[256,96,96]{2,1,0:T(8,128)} %gather_fusion.1, f32[256,96]{1,0:T(8,128)S(1)} %copy.85, pred[256]{0:T(512)(128)(4,1)S(1)} %compare_and_fusion.5), kind=kLoop, calls=%fused_computation.9.clone.1 | loop fusion | flops 7053312 | bytes 9634048 | tf_op jit(solution)/shard_map/while
  326.2 8.3 %multiply_reduce_fusion.5 = f32[256,96]{1,0:T(8,128)S(1)} fusion(f32[256,96,96]{2,1,0:T(8,128)} %gather_fusion.1, f32[256,96]{1,0:T(8,128)S(1)} %copy.85, pred[256]{0:T(512)(128)(4,1)S(1)} %compare_and_fusion.5), kind=kLoop, calls=%fused_computation.9.clone.1 | loop fusion | flops 7053312 | bytes 9634048 | tf_op jit(solution)/shard_map/while
  342.2 8.3 %multiply_reduce_fusion.5 = f32[256,96]{1,0:T(8,128)S(1)} fusion(f32[256,96,96]{2,1,0:T(8,128)} %gather_fusion.1, f32[256,96]{1,0:T(8,128)S(1)} %copy.85, pred[256]{0:T(512)(128)(4,1)S(1)} %compare_and_fusion.5), kind=kLoop, calls=%fused_computation.9.clone.1 | loop fusion | flops 7053312 | bytes 9634048 | tf_op jit(solution)/shard_map/while
  358.2 8.3 %multiply_reduce_fusion.5 = f32[256,96]{1,0:T(8,128)S(1)} fusion(f32[256,96,96]{2,1,0:T(8,128)} %gather_fusion.1, f32[256,96]{1,0:T(8,128)S(1)} %copy.85, pred[256]{0:T(512)(128)(4,1)S(1)} %compare_and_fusion.5), kind=kLoop, calls=%fused_computation.9.clone.1 | loop fusion | flops 7053312 | bytes 9634048 | tf_op jit(solution)/shard_map/while
  376.1 9.5 %all-to-all-done.4 = f32[96,4,512]{2,0,1:T(8,128)S(1)} async-done(((f32[96,4,512]{2,0,1:T(8,128)}), f32[96,4,512]{2,0,1:T(8,128)S(1)}, u32[]{:S(2)}, u32[]{:S(2)}) %all-to-all-start.4) | async-done | bytes 786464 | tf_op jit(solution)/shard_map/all_to_all | solution.py:61
  387.3 29.7 %psum.15 = f32[96]{0:T(128)S(1)} all-reduce(f32[96]{0:T(128)S(1)} %get-tuple-element.95), channel_id=1, replica_groups=mesh['scen'=2,'dw'=4,'reg'=4] {'dw','reg'}, use_global_device_ids=true, to_apply=%region_7.9 | all-reduce | flops 96 | bytes 768 | tf_op jit(solution)/shard_map/psum | solution.py:65
  (185 shorter events, 117.7 us)
Async XLA Ops:
  11.9 15.1 %all-to-all-start.1 = ((f32[96,4,512]{2,0,1:T(8,128)}), f32[96,4,512]{2,0,1:T(8,128)S(1)}, u32[]{:S(2)}, u32[]{:S(2)}) async-start(f32[96,4,512]{2,0,1:T(8,128)} %bitcast.64), calls=%async_computation.1 | async-start | bytes 1572864 | tf_op jit(solution)/shard_map/all_to_all | solution.py:58
  29.6 148.1 %copy-start.3 = (s32[16]{0:T(128)S(1)}, s32[16]{0:T(128)}, u32[]{:S(2)}) copy-start(s32[16]{0:T(128)} %param.19) | copy-start | bytes 196
  29.6 162.0 %copy-start.1 = (f32[16,96]{1,0:T(8,128)S(1)}, f32[16,96]{1,0:T(8,128)}, u32[]{:S(2)}) copy-start(f32[16,96]{1,0:T(8,128)} %param.20) | copy-start | bytes 18436
  166.0 68.5 %copy-start.2 = (f32[96]{0:T(128)S(1)}, f32[96]{0:T(128)}, u32[]{:S(2)}) copy-start(f32[96]{0:T(128)} %param.21) | copy-start | bytes 1156
  166.0 73.3 %copy-start = (f32[64,96,96]{2,1,0:T(8,128)S(1)}, f32[64,96,96]{2,1,0:T(8,128)}, u32[]{:S(2)}) copy-start(f32[64,96,96]{2,1,0:T(8,128)} %get-tuple-element.199) | copy-start | bytes 7077892
  173.4 15.9 %all-to-all-start.2 = ((f32[96,4,512]{2,0,1:T(8,128)}), f32[96,4,512]{2,0,1:T(8,128)}, u32[]{:S(2)}, u32[]{:S(2)}) async-start(f32[96,4,512]{2,0,1:T(8,128)} %copy.36), calls=%async_computation.2 | async-start | bytes 1572864 | tf_op jit(solution)/shard_map/all_to_all | solution.py:61
  193.5 41.0 %all-to-all-start.3 = ((f32[96,4,512]{2,0,1:T(8,128)}), f32[96,4,512]{2,0,1:T(8,128)}, u32[]{:S(2)}, u32[]{:S(2)}) async-start(f32[96,4,512]{2,0,1:T(8,128)} %bitcast.91), calls=%async_computation.3 | async-start | bytes 1572864 | tf_op jit(solution)/shard_map/all_to_all | solution.py:58
  370.4 15.1 %all-to-all-start.4 = ((f32[96,4,512]{2,0,1:T(8,128)}), f32[96,4,512]{2,0,1:T(8,128)S(1)}, u32[]{:S(2)}, u32[]{:S(2)}) async-start(f32[96,4,512]{2,0,1:T(8,128)} %copy.44), calls=%async_computation.4 | async-start | bytes 1572864 | tf_op jit(solution)/shard_map/all_to_all | solution.py:61
where the time goes:
time: 419 us; the launch traced here: 417 us
  local copies, waits for them, and re-layouts  152 us (36%)
  other arithmetic  140 us (33%)
  blocking collectives  72.1 us (17%)
  waiting for transfers between devices  31.3 us (7%)
  starting transfers between devices  15.4 us (4%)
  matrix products  5.55 us (1%)
    while x16, other arithmetic  132 us
    gather x16, local copies, waits for them, and re-layouts, one_block(): picked = jnp.take(kkt_inverse, labels, axis=0)  110 us
    psum x2, blocking collectives, on_device(): system_load = lax.psum(jnp.sum(feeder_loads, axis=0), ('dw', 'reg'))  64.3 us
    all_to_all x2, waiting for transfers between devices, on_device(): lax.all_to_all(roster, 'dw', split_axis=1, concat_axis=1, tiled=True)  21.1 us
    dynamic_update_slice x16, local copies, waits for them, and re-layouts, apply_inverse(): out_blocks = lax.map(one_block, (labels_in, blocks_in))  10.5 us
    all_to_all x2, waiting for transfers between devices, on_device(): lax.all_to_all(owner_rows, 'dw', split_axis=1, concat_axis=1, tiled=True)  10.2 us
    while x24, local copies, waits for them, and re-layouts  8.65 us
  transfers between devices with their start and end apart: 4, of which 3 were waited for; matrix products, arithmetic and copies ran while one was open for 1% of the time, Pallas kernels for 0%

commit v1 on v0

--- a/solution.py
+++ b/solution.py
@@ -62,7 +62,7 @@
         feeder_loads = lax.dot_general(
             owner_table, arrived_loads, contract_rows, precision=lax.Precision.HIGHEST
         )
-        system_load = lax.psum(jnp.sum(feeder_loads, axis=0), ("dw", "reg"))
+        system_load = lax.psum(lax.psum(jnp.sum(feeder_loads, axis=0), "reg"), "dw")
         feeder_duals = jnp.maximum(
             feeder_duals + dual_rate * (feeder_loads - cap_value[:, None]), 0.0
         )

time: 419 us -> 387 us (0.924)
  blocking collectives: 72.1 us -> 39.6 us
    psum x2 -> x4, blocking collectives: 64.3 us -> 31.8 us  [on_device(): system_load = lax.psum(lax.psum(jnp.sum(feeder_loads, axis=0), 'reg'), 'dw')]
where the time goes in v1:
time: 387 us; the launch traced here: 385 us
  local copies, waits for them, and re-layouts  152 us (39%)
  other arithmetic  140 us (36%)
  blocking collectives  39.6 us (10%)
  waiting for transfers between devices  31.3 us (8%)
  starting transfers between devices  15.4 us (4%)
  matrix products  5.55 us (1%)
    while x16, other arithmetic  132 us
    gather x16, local copies, waits for them, and re-layouts, one_block(): picked = jnp.take(kkt_inverse, labels, axis=0)  110 us
    psum x4, blocking collectives, on_device(): system_load = lax.psum(lax.psum(jnp.sum(feeder_loads, axis=0), 'reg'), 'dw')  31.8 us
    all_to_all x2, waiting for transfers between devices, on_device(): lax.all_to_all(roster, 'dw', split_axis=1, concat_axis=1, tiled=True)  21.1 us
    dynamic_update_slice x16, local copies, waits for them, and re-layouts, apply_inverse(): out_blocks = lax.map(one_block, (labels_in, blocks_in))  10.5 us
    all_to_all x2, waiting for transfers between devices, on_device(): lax.all_to_all(owner_rows, 'dw', split_axis=1, concat_axis=1, tiled=True)  10.2 us
    while x24, local copies, waits for them, and re-layouts  8.65 us
    all_to_all x1, blocking collectives, on_device(): lax.all_to_all(local_label, 'dw', split_axis=0, concat_axis=0, tiled=True)  7.81 us
  transfers between devices with their start and end apart: 4, of which 3 were waited for; matrix products, arithmetic and copies ran while one was open for 1% of the time, Pallas kernels for 0%

profile of v1, /device:TPU:0, one launch (start us, length us, event | category | flops | bytes accessed | tf_op | source)
XLA Modules:
  0.0 385.0 jit_solution(650307552702069709)
XLA Ops:
  1.3 7.8 %all_to_all.51 = s32[4,512,1]{1,2,0:T(1,128)S(1)} all-to-all(s32[4,512,1]{1,2,0:T(1,128)S(1)} %bitcast.121), channel_id=1, replica_groups=mesh['scen'=2,'dw'=4,'reg'=4] {'dw'}, dimensions={0} | all-to-all | bytes 16384 | tf_op jit(solution)/shard_map/all_to_all | solution.py:50
  16.9 10.2 %all-to-all-done.1 = f32[96,4,512]{2,0,1:T(8,128)S(1)} async-done(((f32[96,4,512]{2,0,1:T(8,128)}), f32[96,4,512]{2,0,1:T(8,128)S(1)}, u32[]{:S(2)}, u32[]{:S(2)}) %all-to-all-start.1) | async-done | bytes 786464 | tf_op jit(solution)/shard_map/all_to_all | solution.py:58
  29.6 136.5 %while.20 = (s32[]{:T(128)}, f32[8,96,256]{2,1,0:T(8,128)}, f32[8,96,256]{2,0,1:T(8,128)S(1)}, s32[8,256]{1,0:T(8,128)S(1)}, f32[64,96,96]{2,1,0:T(8,128)}, /*index=5*/s32[]{:T(128)}) while((s32[]{:T(128)}, f32[8,96,256]{2,1,0:T(8,128)}, f32[8,96,256]{2,0,1:T(8,128)S(1)}, s32[8,256]{1,0:T(8,128)S(1)}, f32[64,96,96]{2,1,0:T(8,128)}, ...), condition=%wide.region_1.3_spmd, body=%wide.region_0.2_spmd.sunk | while | flops 7056642 | bytes 29306956 | solution.py:24
  29.6 7.8 %gather_fusion = f32[256,96,96]{2,1,0:T(8,128)} fusion(f32[64,96,96]{2,1,0:T(8,128)} %get-tuple-element.179, s32[1024]{0:T(1024)S(1)} %pad_clamp_fusion.4), kind=kCustom, calls=%fused_computation.clone.clone.1 | custom fusion | bytes 18875392 | tf_op jit(solution)/shard_map/while/body/eval_jaxpr/jit(_take)/gather | solution.py:21
  37.6 8.3 %multiply_reduce_fusion.4 = f32[256,96]{1,0:T(8,128)S(1)} fusion(f32[256,96,96]{2,1,0:T(8,128)} %gather_fusion, f32[256,96]{1,0:T(8,128)S(1)} %bitcast.87, pred[256]{0:T(512)(128)(4,1)S(1)} %compare_and_fusion.4), kind=kLoop, calls=%fused_computation.2.clone.1 | loop fusion | flops 7053312 | bytes 9634048 | tf_op jit(solution)/shard_map/while
  46.7 7.8 %gather_fusion = f32[256,96,96]{2,1,0:T(8,128)} fusion(f32[64,96,96]{2,1,0:T(8,128)} %get-tuple-element.179, s32[1024]{0:T(1024)S(1)} %pad_clamp_fusion.4), kind=kCustom, calls=%fused_computation.clone.clone.1 | custom fusion | bytes 18875392 | tf_op jit(solution)/shard_map/while/body/eval_jaxpr/jit(_take)/gather | solution.py:21
  54.7 8.3 %multiply_reduce_fusion.4 = f32[256,96]{1,0:T(8,128)S(1)} fusion(f32[256,96,96]{2,1,0:T(8,128)} %gather_fusion, f32[256,96]{1,0:T(8,128)S(1)} %bitcast.87, pred[256]{0:T(512)(128)(4,1)S(1)} %compare_and_fusion.4), kind=kLoop, calls=%fused_computation.2.clone.1 | loop fusion | flops 7053312 | bytes 9634048 | tf_op jit(solution)/shard_map/while
  63.7 7.8 %gather_fusion = f32[256,96,96]{2,1,0:T(8,128)} fusion(f32[64,96,96]{2,1,0:T(8,128)} %get-tuple-element.179, s32[1024]{0:T(1024)S(1)} %pad_clamp_fusion.4), kind=kCustom, calls=%fused_computation.clone.clone.1 | custom fusion | bytes 18875392 | tf_op jit(solution)/shard_map/while/body/eval_jaxpr/jit(_take)/gather | solution.py:21
  71.7 8.3 %multiply_reduce_fusion.4 = f32[256,96]{1,0:T(8,128)S(1)} fusion(f32[256,96,96]{2,1,0:T(8,128)} %gather_fusion, f32[256,96]{1,0:T(8,128)S(1)} %bitcast.87, pred[256]{0:T(512)(128)(4,1)S(1)} %compare_and_fusion.4), kind=kLoop, calls=%fused_computation.2.clone.1 | loop fusion | flops 7053312 | bytes 9634048 | tf_op jit(solution)/shard_map/while
  80.8 7.8 %gather_fusion = f32[256,96,96]{2,1,0:T(8,128)} fusion(f32[64,96,96]{2,1,0:T(8,128)} %get-tuple-element.179, s32[1024]{0:T(1024)S(1)} %pad_clamp_fusion.4), kind=kCustom, calls=%fused_computation.clone.clone.1 | custom fusion | bytes 18875392 | tf_op jit(solution)/shard_map/while/body/eval_jaxpr/jit(_take)/gather | solution.py:21
  88.8 8.3 %multiply_reduce_fusion.4 = f32[256,96]{1,0:T(8,128)S(1)} fusion(f32[256,96,96]{2,1,0:T(8,128)} %gather_fusion, f32[256,96]{1,0:T(8,128)S(1)} %bitcast.87, pred[256]{0:T(512)(128)(4,1)S(1)} %compare_and_fusion.4), kind=kLoop, calls=%fused_computation.2.clone.1 | loop fusion | flops 7053312 | bytes 9634048 | tf_op jit(solution)/shard_map/while
  97.8 7.8 %gather_fusion = f32[256,96,96]{2,1,0:T(8,128)} fusion(f32[64,96,96]{2,1,0:T(8,128)} %get-tuple-element.179, s32[1024]{0:T(1024)S(1)} %pad_clamp_fusion.4), kind=kCustom, calls=%fused_computation.clone.clone.1 | custom fusion | bytes 18875392 | tf_op jit(solution)/shard_map/while/body/eval_jaxpr/jit(_take)/gather | solution.py:21
  105.8 8.3 %multiply_reduce_fusion.4 = f32[256,96]{1,0:T(8,128)S(1)} fusion(f32[256,96,96]{2,1,0:T(8,128)} %gather_fusion, f32[256,96]{1,0:T(8,128)S(1)} %bitcast.87, pred[256]{0:T(512)(128)(4,1)S(1)} %compare_and_fusion.4), kind=kLoop, calls=%fused_computation.2.clone.1 | loop fusion | flops 7053312 | bytes 9634048 | tf_op jit(solution)/shard_map/while
  114.9 7.8 %gather_fusion = f32[256,96,96]{2,1,0:T(8,128)} fusion(f32[64,96,96]{2,1,0:T(8,128)} %get-tuple-element.179, s32[1024]{0:T(1024)S(1)} %pad_clamp_fusion.4), kind=kCustom, calls=%fused_computation.clone.clone.1 | custom fusion | bytes 18875392 | tf_op jit(solution)/shard_map/while/body/eval_jaxpr/jit(_take)/gather | solution.py:21
  122.9 8.3 %multiply_reduce_fusion.4 = f32[256,96]{1,0:T(8,128)S(1)} fusion(f32[256,96,96]{2,1,0:T(8,128)} %gather_fusion, f32[256,96]{1,0:T(8,128)S(1)} %bitcast.87, pred[256]{0:T(512)(128)(4,1)S(1)} %compare_and_fusion.4), kind=kLoop, calls=%fused_computation.2.clone.1 | loop fusion | flops 7053312 | bytes 9634048 | tf_op jit(solution)/shard_map/while
  131.9 7.8 %gather_fusion = f32[256,96,96]{2,1,0:T(8,128)} fusion(f32[64,96,96]{2,1,0:T(8,128)} %get-tuple-element.179, s32[1024]{0:T(1024)S(1)} %pad_clamp_fusion.4), kind=kCustom, calls=%fused_computation.clone.clone.1 | custom fusion | bytes 18875392 | tf_op jit(solution)/shard_map/while/body/eval_jaxpr/jit(_take)/gather | solution.py:21
  140.0 8.3 %multiply_reduce_fusion.4 = f32[256,96]{1,0:T(8,128)S(1)} fusion(f32[256,96,96]{2,1,0:T(8,128)} %gather_fusion, f32[256,96]{1,0:T(8,128)S(1)} %bitcast.87, pred[256]{0:T(512)(128)(4,1)S(1)} %compare_and_fusion.4), kind=kLoop, calls=%fused_computation.2.clone.1 | loop fusion | flops 7053312 | bytes 9634048 | tf_op jit(solution)/shard_map/while
  149.0 7.8 %gather_fusion = f32[256,96,96]{2,1,0:T(8,128)} fusion(f32[64,96,96]{2,1,0:T(8,128)} %get-tuple-element.179, s32[1024]{0:T(1024)S(1)} %pad_clamp_fusion.4), kind=kCustom, calls=%fused_computation.clone.clone.1 | custom fusion | bytes 18875392 | tf_op jit(solution)/shard_map/while/body/eval_jaxpr/jit(_take)/gather | solution.py:21
  157.0 8.3 %multiply_reduce_fusion.4 = f32[256,96]{1,0:T(8,128)S(1)} fusion(f32[256,96,96]{2,1,0:T(8,128)} %gather_fusion, f32[256,96]{1,0:T(8,128)S(1)} %bitcast.87, pred[256]{0:T(512)(128)(4,1)S(1)} %compare_and_fusion.4), kind=kLoop, calls=%fused_computation.2.clone.1 | loop fusion | flops 7053312 | bytes 9634048 | tf_op jit(solution)/shard_map/while
  177.6 11.7 %all-to-all-done.2 = f32[96,4,512]{2,0,1:T(8,128)} async-done(((f32[96,4,512]{2,0,1:T(8,128)}), f32[96,4,512]{2,0,1:T(8,128)}, u32[]{:S(2)}, u32[]{:S(2)}) %all-to-all-start.2) | async-done | bytes 786464 | tf_op jit(solution)/shard_map/all_to_all | solution.py:61
  199.9 11.9 %psum.28 = f32[96]{0:T(128)S(1)} all-reduce(f32[96]{0:T(128)S(1)} %get-tuple-element.99), channel_id=1, replica_groups=mesh['scen'=2,'dw'=4,'reg'=4] {'reg'}, use_global_device_ids=true, to_apply=%region_3.5 | all-reduce | flops 96 | bytes 768 | tf_op jit(solution)/shard_map/psum | solution.py:65
  222.4 127.9 %while.21 = (s32[]{:T(128)}, f32[8,96,256]{2,1,0:T(8,128)}, f32[8,96,256]{2,1,0:T(8,128)}, s32[8,256]{1,0:T(8,128)S(1)}, f32[64,96,96]{2,1,0:T(8,128)S(1)}, /*index=5*/s32[]{:T(128)}) while((s32[]{:T(128)}, f32[8,96,256]{2,1,0:T(8,128)}, f32[8,96,256]{2,1,0:T(8,128)}, s32[8,256]{1,0:T(8,128)S(1)}, f32[64,96,96]{2,1,0:T(8,128)S(1)}, ...), condition=%wide.region_6.8_spmd, body=%wide.region_5.7_spmd.sunk | while | flops 7056642 | bytes 29306956 | solution.py:24
  229.4 8.3 %multiply_reduce_fusion.5 = f32[256,96]{1,0:T(8,128)S(1)} fusion(f32[256,96,96]{2,1,0:T(8,128)} %gather_fusion.1, f32[256,96]{1,0:T(8,128)S(1)} %copy.85, pred[256]{0:T(512)(128)(4,1)S(1)} %compare_and_fusion.5), kind=kLoop, calls=%fused_computation.9.clone.1 | loop fusion | flops 7053312 | bytes 9634048 | tf_op jit(solution)/shard_map/while
  245.4 8.3 %multiply_reduce_fusion.5 = f32[256,96]{1,0:T(8,128)S(1)} fusion(f32[256,96,96]{2,1,0:T(8,128)} %gather_fusion.1, f32[256,96]{1,0:T(8,128)S(1)} %copy.85, pred[256]{0:T(512)(128)(4,1)S(1)} %compare_and_fusion.5), kind=kLoop, calls=%fused_computation.9.clone.1 | loop fusion | flops 7053312 | bytes 9634048 | tf_op jit(solution)/shard_map/while
  261.4 8.3 %multiply_reduce_fusion.5 = f32[256,96]{1,0:T(8,128)S(1)} fusion(f32[256,96,96]{2,1,0:T(8,128)} %gather_fusion.1, f32[256,96]{1,0:T(8,128)S(1)} %copy.85, pred[256]{0:T(512)(128)(4,1)S(1)} %compare_and_fusion.5), kind=kLoop, calls=%fused_computation.9.clone.1 | loop fusion | flops 7053312 | bytes 9634048 | tf_op jit(solution)/shard_map/while
  277.3 8.3 %multiply_reduce_fusion.5 = f32[256,96]{1,0:T(8,128)S(1)} fusion(f32[256,96,96]{2,1,0:T(8,128)} %gather_fusion.1, f32[256,96]{1,0:T(8,128)S(1)} %copy.85, pred[256]{0:T(512)(128)(4,1)S(1)} %compare_and_fusion.5), kind=kLoop, calls=%fused_computation.9.clone.1 | loop fusion | flops 7053312 | bytes 9634048 | tf_op jit(solution)/shard_map/while
  293.3 8.3 %multiply_reduce_fusion.5 = f32[256,96]{1,0:T(8,128)S(1)} fusion(f32[256,96,96]{2,1,0:T(8,128)} %gather_fusion.1, f32[256,96]{1,0:T(8,128)S(1)} %copy.85, pred[256]{0:T(512)(128)(4,1)S(1)} %compare_and_fusion.5), kind=kLoop, calls=%fused_computation.9.clone.1 | loop fusion | flops 7053312 | bytes 9634048 | tf_op jit(solution)/shard_map/while
  309.3 8.3 %multiply_reduce_fusion.5 = f32[256,96]{1,0:T(8,128)S(1)} fusion(f32[256,96,96]{2,1,0:T(8,128)} %gather_fusion.1, f32[256,96]{1,0:T(8,128)S(1)} %copy.85, pred[256]{0:T(512)(128)(4,1)S(1)} %compare_and_fusion.5), kind=kLoop, calls=%fused_computation.9.clone.1 | loop fusion | flops 7053312 | bytes 9634048 | tf_op jit(solution)/shard_map/while
  325.3 8.3 %multiply_reduce_fusion.5 = f32[256,96]{1,0:T(8,128)S(1)} fusion(f32[256,96,96]{2,1,0:T(8,128)} %gather_fusion.1, f32[256,96]{1,0:T(8,128)S(1)} %copy.85, pred[256]{0:T(512)(128)(4,1)S(1)} %compare_and_fusion.5), kind=kLoop, calls=%fused_computation.9.clone.1 | loop fusion | flops 7053312 | bytes 9634048 | tf_op jit(solution)/shard_map/while
  341.3 8.3 %multiply_reduce_fusion.5 = f32[256,96]{1,0:T(8,128)S(1)} fusion(f32[256,96,96]{2,1,0:T(8,128)} %gather_fusion.1, f32[256,96]{1,0:T(8,128)S(1)} %copy.85, pred[256]{0:T(512)(128)(4,1)S(1)} %compare_and_fusion.5), kind=kLoop, calls=%fused_computation.9.clone.1 | loop fusion | flops 7053312 | bytes 9634048 | tf_op jit(solution)/shard_map/while
  359.2 9.5 %all-to-all-done.4 = f32[96,4,512]{2,0,1:T(8,128)S(1)} async-done(((f32[96,4,512]{2,0,1:T(8,128)}), f32[96,4,512]{2,0,1:T(8,128)S(1)}, u32[]{:S(2)}, u32[]{:S(2)}) %all-to-all-start.4) | async-done | bytes 786464 | tf_op jit(solution)/shard_map/all_to_all | solution.py:61
  370.4 8.3 %psum.30 = f32[96]{0:T(128)S(1)} all-reduce(f32[96]{0:T(128)S(1)} %get-tuple-element.95), channel_id=1, replica_groups=mesh['scen'=2,'dw'=4,'reg'=4] {'reg'}, use_global_device_ids=true, to_apply=%region_8.10 | all-reduce | flops 96 | bytes 768 | tf_op jit(solution)/shard_map/psum | solution.py:65
  (187 shorter events, 129.3 us)
Async XLA Ops:
  11.9 15.1 %all-to-all-start.1 = ((f32[96,4,512]{2,0,1:T(8,128)}), f32[96,4,512]{2,0,1:T(8,128)S(1)}, u32[]{:S(2)}, u32[]{:S(2)}) async-start(f32[96,4,512]{2,0,1:T(8,128)} %bitcast.64), calls=%async_computation.1 | async-start | bytes 1572864 | tf_op jit(solution)/shard_map/all_to_all | solution.py:58
  29.6 148.1 %copy-start.3 = (s32[16]{0:T(128)S(1)}, s32[16]{0:T(128)}, u32[]{:S(2)}) copy-start(s32[16]{0:T(128)} %param.19) | copy-start | bytes 196
  29.6 162.0 %copy-start.1 = (f32[16,96]{1,0:T(8,128)S(1)}, f32[16,96]{1,0:T(8,128)}, u32[]{:S(2)}) copy-start(f32[16,96]{1,0:T(8,128)} %param.20) | copy-start | bytes 18436
  166.0 51.6 %copy-start.2 = (f32[96]{0:T(128)S(1)}, f32[96]{0:T(128)}, u32[]{:S(2)}) copy-start(f32[96]{0:T(128)} %param.21) | copy-start | bytes 1156
  166.0 56.4 %copy-start = (f32[64,96,96]{2,1,0:T(8,128)S(1)}, f32[64,96,96]{2,1,0:T(8,128)}, u32[]{:S(2)}) copy-start(f32[64,96,96]{2,1,0:T(8,128)} %get-tuple-element.199) | copy-start | bytes 7077892
  173.4 15.9 %all-to-all-start.2 = ((f32[96,4,512]{2,0,1:T(8,128)}), f32[96,4,512]{2,0,1:T(8,128)}, u32[]{:S(2)}, u32[]{:S(2)}) async-start(f32[96,4,512]{2,0,1:T(8,128)} %copy.36), calls=%async_computation.2 | async-start | bytes 1572864 | tf_op jit(solution)/shard_map/all_to_all | solution.py:61
  193.5 24.1 %all-to-all-start.3 = ((f32[96,4,512]{2,0,1:T(8,128)}), f32[96,4,512]{2,0,1:T(8,128)}, u32[]{:S(2)}, u32[]{:S(2)}) async-start(f32[96,4,512]{2,0,1:T(8,128)} %bitcast.91), calls=%async_computation.3 | async-start | bytes 1572864 | tf_op jit(solution)/shard_map/all_to_all | solution.py:58
  353.5 15.1 %all-to-all-start.4 = ((f32[96,4,512]{2,0,1:T(8,128)}), f32[96,4,512]{2,0,1:T(8,128)S(1)}, u32[]{:S(2)}, u32[]{:S(2)}) async-start(f32[96,4,512]{2,0,1:T(8,128)} %copy.44), calls=%async_computation.4 | async-start | bytes 1572864 | tf_op jit(solution)/shard_map/all_to_all | solution.py:61
